TPU v7x, 32 devices: a whole 2x2x4 slice. The times are simulated.
32 devices in a mesh: az: 8 (over z, x), rx: 4 (over y, core).
Axes of the slice: x: 2, y: 2, z: 4, core: 2. Of those that a mesh axis runs over, the one named last changes fastest.
Arguments:
- adjoint: float32 [5, 8, 128, 512], P(None, 'az', None, 'rx'), may hold values from -6 to 6
- density: float32 [8, 128, 512], P('az', None, 'rx'), may hold values from 0.6 to 1.4
- velocity: float32 [3, 8, 128, 512], P(None, 'az', None, 'rx'), may hold values from -0.9 to 0.9
- pressure: float32 [8, 128, 512], P('az', None, 'rx'), may hold values from 0.5 to 0.9
- fwh_cell: int32 [8, 4, 256], P('az', 'rx'), may hold values from 0 to 16383
- fwh_bin: int32 [8, 4, 256], P('az', 'rx'), may hold values from 0 to 255
- fwh_weight: float32 [8, 4, 256], P('az', 'rx'), may hold values from -6 to 6
- fwh_count: int32 [8, 4], P('az', 'rx'), may hold values from 1 to 256, as said below
Outputs:
- section: float32 [5, 8, 128, 512], P(None, 'az', None, 'rx')
- signal: float32 [256], P(('az', 'rx'))
Inputs may be any that keep to these rules, and one draw needn't show every extreme that they name: `fwh_count`: slots at or after a device's count are unused; some device has all 256 slots live.
All inputs are finite; a program needn't handle non-finite values.
Results may differ from a plain program's by a relative error of at most 0.00017.
Values sent between devices are 32-bit elements; how exact they have to be, the bound alone decides.
No kernel may reach another device: no remote copies, remote signals or barrier semaphores. Data moves between devices by JAX's collectives and lax.ppermute only.
A program may use at most 64 MiB of HBM per device.

v0:
```python
import math
import jax
import jax.numpy as jnp
from jax import lax
from jax.sharding import PartitionSpec as P

BIN_DEV = 8
ALPHA_FILTER = 0.495
COEF_ZERO = 11.0 / 16.0 + 5.0 * ALPHA_FILTER / 8.0
COEF_ONE = 15.0 / 32.0 + 17.0 * ALPHA_FILTER / 16.0
COEF_TWO = -3.0 / 16.0 + 3.0 * ALPHA_FILTER / 8.0
COEF_THREE = 1.0 / 32.0 - ALPHA_FILTER / 16.0
ALPHA_DERIV = 1.0 / 3.0
NEAR_COEF = 14.0 / 9.0
FAR_COEF = 1.0 / 9.0
AXIAL_STEP = 0.02
RADIAL_STEP = 0.02
INNER_RADIUS = 0.3
SECTION_STEP = 0.004
GAMMA_GAS = 1.4


def padded_2(shard, sides, width):
    for axis, dim in sides:
        size, length = (lax.axis_size(axis), shard.shape[dim])
        up = [(i, (i + 1) % size) for i in range(size - 1)]
        down = [(j, i) for i, j in up]
        last = lax.slice_in_dim(shard, length - width, length, axis=dim)
        leading = lax.slice_in_dim(shard, 0, width, axis=dim)
        before = lax.ppermute(last, axis, up)
        after = lax.ppermute(leading, axis, down)
        shard = jnp.concatenate([before, shard, after], axis=dim)
    return shard


def mode_gains(count):
    angle = jnp.arange(count, dtype=jnp.int32).astype(jnp.float32) * (2.0 * math.pi / count)
    cosine = jnp.cos(angle)
    filter_gain = (
        COEF_ZERO
        + COEF_ONE * cosine
        + COEF_TWO * jnp.cos(2.0 * angle)
        + COEF_THREE * jnp.cos(3.0 * angle)
    ) / (1.0 + 2.0 * ALPHA_FILTER * cosine)
    spacing = 2.0 * math.pi / count
    deriv_gain = (
        filter_gain
        * (NEAR_COEF * jnp.sin(angle) + 0.5 * FAR_COEF * jnp.sin(2.0 * angle))
        / (spacing * (1.0 + 2.0 * ALPHA_DERIV * cosine))
    )
    return (filter_gain, deriv_gain)


def kernel_values(offsets, count, filter_gain, deriv_gain):
    modes = jnp.arange(count, dtype=jnp.int32)
    phase = jnp.mod(offsets[..., None] * modes, count).astype(jnp.float32) * (2.0 * math.pi / count)
    smooth = jnp.sum(filter_gain * jnp.cos(phase), axis=-1) / count
    slope = -jnp.sum(deriv_gain * jnp.sin(phase), axis=-1) / count
    return (smooth, slope)


def central(padded, axis, width, step):

    def piece_at(start):
        return lax.slice_in_dim(padded, start, start + width, axis=axis)

    return (
        45.0 * (piece_at(4) - piece_at(2))
        - 9.0 * (piece_at(5) - piece_at(1))
        + (piece_at(6) - piece_at(0))
    ) / (60.0 * step)


def adjoint_flux(grad_axial, grad_radial, grad_theta, density, velocity, pressure):
    axial_vel, radial_vel, swirl_vel = (velocity[0], velocity[1], velocity[2])
    stiff = GAMMA_GAS * pressure
    inverse = 1.0 / density
    mass_term = axial_vel * grad_axial[0] + radial_vel * grad_radial[0] + swirl_vel * grad_theta[0]
    axial_term = (
        density * grad_axial[0]
        + axial_vel * grad_axial[1]
        + stiff * grad_axial[4]
        + radial_vel * grad_radial[1]
        + swirl_vel * grad_theta[1]
    )
    radial_term = (
        axial_vel * grad_axial[2]
        + density * grad_radial[0]
        + radial_vel * grad_radial[2]
        + stiff * grad_radial[4]
        + swirl_vel * grad_theta[2]
    )
    swirl_term = (
        axial_vel * grad_axial[3]
        + radial_vel * grad_radial[3]
        + density * grad_theta[0]
        + swirl_vel * grad_theta[3]
        + stiff * grad_theta[4]
    )
    energy_term = (
        inverse * grad_axial[1]
        + axial_vel * grad_axial[4]
        + inverse * grad_radial[2]
        + radial_vel * grad_radial[4]
        + inverse * grad_theta[3]
        + swirl_vel * grad_theta[4]
    )
    return jnp.stack([mass_term, axial_term, radial_term, swirl_term, energy_term])


def local(adjoint, density, velocity, pressure, fwh_cell, fwh_bin, fwh_weight, fwh_count):
    fields, local_theta, radial_cells, axial_cells = adjoint.shape
    count = local_theta * lax.axis_size("az")
    filter_gain, deriv_gain = mode_gains(count)
    piece = lax.all_gather(adjoint, "az", axis=1, tiled=True)
    width = piece.shape[1]
    targets = lax.axis_index("az") * local_theta + jnp.arange(local_theta, dtype=jnp.int32)
    sources = jnp.arange(width, dtype=jnp.int32)
    offsets = jnp.mod(targets[:, None] - sources[None, :], count)
    smooth, slope = kernel_values(offsets, count, filter_gain, deriv_gain)
    filtered = jnp.einsum("ij,cjrx->cirx", smooth, piece, precision=lax.Precision.HIGHEST)
    dtheta = jnp.einsum("ij,cjrx->cirx", slope, piece, precision=lax.Precision.HIGHEST)
    pad_axial = padded_2(filtered, (("rx", 3),), 3)
    daxial = central(pad_axial, 3, axial_cells, AXIAL_STEP)
    pad_radial = jnp.pad(filtered, ((0, 0), (0, 0), (3, 3), (0, 0)))
    dradial = central(pad_radial, 2, radial_cells, RADIAL_STEP)
    radius = (
        INNER_RADIUS
        + (jnp.arange(radial_cells, dtype=jnp.int32).astype(jnp.float32) + 0.5) * RADIAL_STEP
    ).reshape(radial_cells, 1)
    flux = adjoint_flux(daxial, dradial, dtheta / radius, density, velocity, pressure)
    section = filtered + SECTION_STEP * flux
    slot_cells = fwh_cell[0, 0]
    slot_bins = fwh_bin[0, 0]
    slot_weights = fwh_weight[0, 0]
    live = jnp.arange(slot_cells.shape[0], dtype=jnp.int32) < fwh_count[0, 0]
    picked = jnp.take(section.reshape(fields, -1), slot_cells, axis=1)
    values = jnp.where(live, slot_weights * (picked[4] + picked[1]), 0.0)
    totals = jax.ops.segment_sum(
        values, slot_bins, num_segments=BIN_DEV * lax.axis_size("az") * lax.axis_size("rx")
    )
    signal = lax.psum_scatter(totals, ("az", "rx"), scatter_dimension=0, tiled=True)
    return (section, signal)


def solution(mesh):
    placed = (
        P(None, "az", None, "rx"),
        P("az", None, "rx"),
        P(None, "az", None, "rx"),
        P("az", None, "rx"),
        P("az", "rx", None),
        P("az", "rx", None),
        P("az", "rx", None),
        P("az", "rx"),
    )
    return jax.shard_map(
        local,
        mesh=mesh,
        in_specs=placed,
        out_specs=(P(None, "az", None, "rx"), P(("az", "rx"))),
        check_vma=False,
    )
```

profile of v0, /device:TPU:0, one launch (start us, length us, event | category | flops | bytes accessed | tf_op | source)
XLA Modules:
  0.0 143.3 jit_solution(1472916147521559716)
XLA Ops:
  7.2 0.0 all-gather.2.cloned.1.call-start
  7.2 0.7 all-gather.2.cloned.1.call-update
  8.6 0.1 multiply_divide_fusion
  8.6 0.7 compare_select_fusion
  9.3 0.2 multiply_reduce_fusion
  9.6 0.7 compare_and_fusion
  10.3 57.3 %all-gather.2.cloned.1.call-done = f32[5,8,128,128]{3,2,1,0:T(8,128)} async-done(((f32[5,1,128,128]{3,2,1,0:T(8,128)}), f32[5,8,128,128]{3,2,1,0:T(8,128)}) %all-gather.2.cloned.1.call-update) | async-done | bytes 2621456 | tf_op jit(solution)/shard_map/all_gather | solution.py:115
  67.6 5.4 %fusion.2 = f32[1,5,128,128]{3,0,2,1:T(1,128)S(1)} fusion(f32[5,8,128,128]{3,2,1,0:T(8,128)} %all-gather.2.cloned.1.call-done, f32[8]{0:T(128)S(1)} %get-tuple-element.3), kind=kOutput, calls=%fused_computation.4 | convolution fusion | flops 7864328 | bytes 2949152 | tf_op jit(solution)/shard_map/ij,cjrx->cirx/dot_general | solution.py:121
  73.0 0.2 fusion.62
  73.2 1.3 collective-permute-start
  74.5 3.1 %collective-permute-start.1 = (f32[5,1,128,3]{3,2,1,0:T(8,128)S(1)}, f32[5,1,128,3]{3,2,1,0:T(8,128)S(1)}, u32[]{:S(2)}, u32[]{:S(2)}) collective-permute-start(f32[5,1,128,3]{3,2,1,0:T(8,128)S(1)} %get-tuple-element.7), channel_id=1, source_target_pairs={{0,1},{1,2},{2,3},{4,5},{5,6},{6,7},{8,9},{9,10},{10,11},{12,13},{... | collective-permute-start | bytes 23048 | tf_op jit(solution)/shard_map/ppermute | solution.py:30
  77.5 0.0 copy-done
  77.5 0.0 copy-start.1
  77.5 0.0 copy-start.3
  77.6 0.0 copy-start.4
  77.6 3.6 %fusion = f32[1,5,128,128]{3,0,2,1:T(1,128)S(1)} fusion(f32[5,8,128,128]{3,2,1,0:T(8,128)S(1)} %copy-done, f32[8]{0:T(128)S(1)} %get-tuple-element.2), kind=kOutput, calls=%fused_computation.2 | convolution fusion | flops 7864336 | bytes 2949152 | tf_op jit(solution)/shard_map/ij,cjrx->cirx/dot_general | solution.py:122
  81.1 0.1 broadcast_divide_fusion
  81.2 0.0 collective-permute-done
  81.2 0.0 collective-permute-done.1
  81.3 1.1 fusion.9
  82.4 0.0 copy-done.1
  82.5 0.0 copy-done.3
  82.5 0.0 copy-done.4
  82.7 0.0 copy-start.2
  82.7 0.0 copy-start.5
  82.7 4.7 %copy.13 = f32[5,128,128]{0,2,1:T(8,128)} copy(f32[5,128,128]{2,1,0:T(8,128)S(1)} %multiply_add_fusion) | data formatting | bytes 655360 | tf_op jit(solution)/shard_map/add | solution.py:132
  87.4 4.1 %gather_fusion = f32[256,5]{1,0:T(8,128)S(1)} fusion(f32[5,16384]{0,1:T(8,128)} %bitcast.150, s32[1024]{0:T(1024)S(1)} %pad_clamp_fusion), kind=kCustom, calls=%fused_computation | custom fusion | bytes 11264 | tf_op jit(solution)/shard_map/jit(_take)/gather | solution.py:137
  91.5 0.1 select_bitcast_fusion
  91.6 0.2 fusion.16
  91.9 2.5 %scatter_custom_fusion = f32[256]{0:T(256)S(1)} fusion(s32[256]{0:T(256)} %bitcast.159, f32[256]{0:T(256)S(1)} %compare_select_fusion.4, f32[]{:T(128)} %constant.83.clone.1), kind=kCustom, calls=%fused_computation.103 | custom fusion | flops 256 | bytes 1536 | tf_op jit(solution)/shard_map/scatter-add | solution.py:139
  94.3 41.5 %all-reduce.1 = f32[256]{0:T(256)S(1)} all-reduce(f32[256]{0:T(256)S(1)} %scatter_custom_fusion), channel_id=2, replica_groups=mesh['az'=8,'rx'=4] {'az','rx'}, use_global_device_ids=true, to_apply=%region_3.4.clone | all-reduce | flops 256 | bytes 2048
  135.9 0.6 dynamic-slice
  (13 shorter events, 0.3 us)
Async XLA Ops:
  7.2 60.4 %all-gather.2.cloned.1.call-start = ((), (), s32[]{:S(2)}) async-start(), calls=%async_computation | async-start | bytes 2949120 | tf_op jit(solution)/shard_map/all_gather | solution.py:115
  67.6 10.0 %copy-start = (f32[5,8,128,128]{3,2,1,0:T(8,128)S(1)}, f32[5,8,128,128]{3,2,1,0:T(8,128)}, u32[]{:S(2)}) copy-start(f32[5,8,128,128]{3,2,1,0:T(8,128)} %all-gather.2.cloned.1.call-done) | copy-start | bytes 7864324
  73.2 8.1 %collective-permute-start = (f32[5,1,128,3]{3,2,1,0:T(8,128)S(1)}, f32[5,1,128,3]{3,2,1,0:T(8,128)S(1)}, u32[]{:S(2)}, u32[]{:S(2)}) collective-permute-start(f32[5,1,128,3]{3,2,1,0:T(8,128)S(1)} %get-tuple-element.6), channel_id=1, source_target_pairs={{1,0},{2,1},{3,2},{5,4},{6,5},{7,6},{9,8},{10,9},{11,10},{13,12},{... | collective-permute-start | bytes 23048 | tf_op jit(solution)/shard_map/ppermute | solution.py:31
  74.5 6.8 %collective-permute-start.1 = (f32[5,1,128,3]{3,2,1,0:T(8,128)S(1)}, f32[5,1,128,3]{3,2,1,0:T(8,128)S(1)}, u32[]{:S(2)}, u32[]{:S(2)}) collective-permute-start(f32[5,1,128,3]{3,2,1,0:T(8,128)S(1)} %get-tuple-element.7), channel_id=1, source_target_pairs={{0,1},{1,2},{2,3},{4,5},{5,6},{6,7},{8,9},{9,10},{10,11},{12,13},{... | collective-permute-start | bytes 23048 | tf_op jit(solution)/shard_map/ppermute | solution.py:30
  77.5 4.9 %copy-start.1 = (f32[3,1,128,128]{3,2,1,0:T(8,128)S(1)}, f32[3,1,128,128]{3,2,1,0:T(8,128)}, u32[]{:S(2)}) copy-start(f32[3,1,128,128]{3,2,1,0:T(8,128)} %param.10) | copy-start | bytes 589828
  77.5 4.9 %copy-start.3 = (f32[1,128,128]{2,1,0:T(8,128)S(1)}, f32[1,128,128]{2,1,0:T(8,128)}, u32[]{:S(2)}) copy-start(f32[1,128,128]{2,1,0:T(8,128)} %param.9) | copy-start | bytes 196612
  77.6 4.9 %copy-start.4 = (f32[1,128,128]{2,1,0:T(8,128)S(1)}, f32[1,128,128]{2,1,0:T(8,128)}, u32[]{:S(2)}) copy-start(f32[1,128,128]{2,1,0:T(8,128)} %param.11) | copy-start | bytes 196612
  82.7 4.7 %copy-start.2 = (f32[5,128,128]{2,1,0:T(8,128)}, f32[5,128,128]{2,1,0:T(8,128)S(1)}, u32[]{:S(2)}) copy-start(f32[5,128,128]{2,1,0:T(8,128)S(1)} %multiply_add_fusion) | copy-start | bytes 983044
  82.7 9.2 %copy-start.5 = (f32[1,1,256]{2,1,0:T(1,128)S(1)}, f32[1,1,256]{2,1,0:T(1,128)}, u32[]{:S(2)}) copy-start(f32[1,1,256]{2,1,0:T(1,128)} %param.14) | copy-start | bytes 3076
Sparse Core Ops, SparseCore 0:
  10.2 57.3 all-gather.1
where the time goes:
time: 144 us; the launch traced here: 143 us
  waiting for transfers between devices  58 us (40%)
  blocking collectives  41.5 us (29%)
  between operations  14.9 us (10%)
  local copies, waits for them, and re-layouts  9.59 us (7%)
  matrix products  8.98 us (6%)
  other arithmetic  5.92 us (4%)
  starting transfers between devices  4.38 us (3%)
    all_gather x1, waiting for transfers between devices, local(): piece = lax.all_gather(adjoint, 'az', axis=1, tiled=True)  57.3 us
    unnamed x1, blocking collectives  41.5 us
    dot_general x1, matrix products, local(): jnp.einsum('ij,cjrx->cirx', smooth, piece, precision=lax.Precision.HIGHEST)  5.43 us
    add x1, local copies, waits for them, and re-layouts, local(): section = filtered + SECTION_STEP * flux  4.71 us
    gather x1, local copies, waits for them, and re-layouts, local(): picked = jnp.take(section.reshape(fields, -1), slot_cells, axis=1)  4.1 us
    dot_general x1, matrix products, local(): jnp.einsum('ij,cjrx->cirx', slope, piece, precision=lax.Precision.HIGHEST)  3.56 us
    ppermute x1, starting transfers between devices, padded_2(): before = lax.ppermute(last, axis, up)  3.05 us
  transfers between devices with their start and end apart: 3, of which 1 were waited for; matrix products, arithmetic and copies ran while one was open for 4% of the time, Pallas kernels for 0%

commit v1 on v0

--- a/solution.py
+++ b/solution.py
@@ -18,6 +18,19 @@
 INNER_RADIUS = 0.3
 SECTION_STEP = 0.004
 GAMMA_GAS = 1.4
+
+
+def collect(value, axis, dim):
+    ways = lax.axis_size(axis)
+    up = [(d, (d + 1) % ways) for d in range(ways)]
+    down = [(d, (d - 1) % ways) for d in range(ways)]
+    earlier, later = ([value], [value])
+    for _ in range(ways // 2):
+        earlier.append(lax.ppermute(earlier[-1], axis, up))
+    for _ in range((ways - 1) // 2):
+        later.append(lax.ppermute(later[-1], axis, down))
+    line = jnp.concatenate([*earlier[::-1], *later[1:]], axis=dim)
+    return jnp.roll(line, (lax.axis_index(axis) - ways // 2) * value.shape[dim], axis=dim)
 
 
 def padded_2(shard, sides, width):
@@ -112,7 +125,7 @@
     fields, local_theta, radial_cells, axial_cells = adjoint.shape
     count = local_theta * lax.axis_size("az")
     filter_gain, deriv_gain = mode_gains(count)
-    piece = lax.all_gather(adjoint, "az", axis=1, tiled=True)
+    piece = collect(adjoint, "az", 1)
     width = piece.shape[1]
     targets = lax.axis_index("az") * local_theta + jnp.arange(local_theta, dtype=jnp.int32)
     sources = jnp.arange(width, dtype=jnp.int32)

time: 144 us -> 133 us (0.924)
  starting transfers between devices: 4.38 us -> 22.2 us
  waiting for transfers between devices: 58 us -> 41.6 us
  between operations: 14.9 us -> 1.63 us
  local copies, waits for them, and re-layouts: 9.59 us -> 11.2 us
    all_gather x1 -> x0, waiting for transfers between devices: 57.3 us -> none  [local(): piece = lax.all_gather(adjoint, 'az', axis=1, tiled=True)]
    ppermute x0 -> x7, waiting for transfers between devices: none -> 38.6 us  [the longest x4 37.1 us: collect(): earlier.append(lax.ppermute(earlier[-1], axis, up))]
    ppermute x0 -> x7, starting transfers between devices: none -> 18.8 us  [the longest x3 11 us: collect(): later.append(lax.ppermute(later[-1], axis, down))]
    ppermute x1, waiting for transfers between devices: 0.01 us -> 3.03 us  [padded_2(): after = lax.ppermute(leading, axis, down)]
    dot_general x1, matrix products: 5.43 us -> 3.85 us  [local(): jnp.einsum('ij,cjrx->cirx', smooth, piece, precision=lax.Precision.HIGHEST)]
  transfers between devices with their start and end apart: 3 -> 9, of which waited for: 1 -> 6; matrix products, arithmetic and copies ran while one was open for 4% -> 2% of each run, Pallas kernels for 0% -> 0%
where the time goes in v1:
time: 133 us; the launch traced here: 132 us
  blocking collectives  42 us (32%)
  waiting for transfers between devices  41.6 us (31%)
  starting transfers between devices  22.2 us (17%)
  local copies, waits for them, and re-layouts  11.2 us (8%)
  matrix products  7.7 us (6%)
  other arithmetic  5.91 us (4%)
  between operations  1.63 us (1%)
    unnamed x1, blocking collectives  42 us
    ppermute x4, waiting for transfers between devices, collect(): earlier.append(lax.ppermute(earlier[-1], axis, up))  37.1 us
    ppermute x3, starting transfers between devices, collect(): later.append(lax.ppermute(later[-1], axis, down))  11 us
    ppermute x4, starting transfers between devices, collect(): earlier.append(lax.ppermute(earlier[-1], axis, up))  7.85 us
    add x1, local copies, waits for them, and re-layouts, local(): section = filtered + SECTION_STEP * flux  4.69 us
    gather x1, local copies, waits for them, and re-layouts, local(): picked = jnp.take(section.reshape(fields, -1), slot_cells, axis=1)  4.1 us
    dot_general x1, matrix products, local(): jnp.einsum('ij,cjrx->cirx', smooth, piece, precision=lax.Precision.HIGHEST)  3.85 us
    dot_general x1, matrix products, local(): jnp.einsum('ij,cjrx->cirx', slope, piece, precision=lax.Precision.HIGHEST)  3.85 us
  transfers between devices with their start and end apart: 9, of which 6 were waited for; matrix products, arithmetic and copies ran while one was open for 2% of the time, Pallas kernels for 0%

profile of v1, /device:TPU:0, one launch (start us, length us, event | category | flops | bytes accessed | tf_op | source)
XLA Modules:
  0.0 132.3 jit_solution(7361754063797236016)
XLA Ops:
  0.6 3.0 %collective-permute-start = (f32[5,1,128,128]{3,2,1,0:T(8,128)}, f32[5,1,128,128]{3,2,1,0:T(8,128)S(1)}, u32[]{:S(2)}, u32[]{:S(2)}) collective-permute-start(f32[5,1,128,128]{3,2,1,0:T(8,128)} %param.8), channel_id=1, source_target_pairs={{0,4},{4,8},{8,12},{12,16},{16,20},{20,24},{24,28},{28,0},{1,5},{5... | collective-permute-start | bytes 983048 | tf_op jit(solution)/shard_map/ppermute | solution.py:29
  3.6 3.1 %collective-permute-start.4 = (f32[5,1,128,128]{3,2,1,0:T(8,128)}, f32[5,1,128,128]{3,2,1,0:T(8,128)S(1)}, u32[]{:S(2)}, u32[]{:S(2)}) collective-permute-start(f32[5,1,128,128]{3,2,1,0:T(8,128)} %param.8), channel_id=1, source_target_pairs={{0,28},{4,0},{8,4},{12,8},{16,12},{20,16},{24,20},{28,24},{1,29},{... | collective-permute-start | bytes 983048 | tf_op jit(solution)/shard_map/ppermute | solution.py:31
  7.4 10.5 %collective-permute-done = f32[5,1,128,128]{3,2,1,0:T(8,128)S(1)} collective-permute-done((f32[5,1,128,128]{3,2,1,0:T(8,128)}, f32[5,1,128,128]{3,2,1,0:T(8,128)S(1)}, u32[]{:S(2)}, u32[]{:S(2)}) %collective-permute-start) | collective-permute-done | bytes 327712 | tf_op jit(solution)/shard_map/ppermute | solution.py:29
  17.9 2.4 %collective-permute-start.1 = (f32[5,1,128,128]{3,2,1,0:T(8,128)S(1)}, f32[5,1,128,128]{3,2,1,0:T(8,128)S(1)}, u32[]{:S(2)}, u32[]{:S(2)}) collective-permute-start(f32[5,1,128,128]{3,2,1,0:T(8,128)S(1)} %collective-permute-done), channel_id=1, source_target_pairs={{0,4},{4,8},{8,12},{12,16},{16,20},{20,24},{24,28},{28,0},{1,5},{5... | collective-permute-start | bytes 983048 | tf_op jit(solution)/shard_map/ppermute | solution.py:29
  20.3 0.1 multiply_divide_fusion
  20.4 0.7 compare_select_fusion
  21.1 9.1 %collective-permute-done.1 = f32[5,1,128,128]{3,2,1,0:T(8,128)S(1)} collective-permute-done((f32[5,1,128,128]{3,2,1,0:T(8,128)S(1)}, f32[5,1,128,128]{3,2,1,0:T(8,128)S(1)}, u32[]{:S(2)}, u32[]{:S(2)}) %collective-permute-start.1) | collective-permute-done | bytes 327712 | tf_op jit(solution)/shard_map/ppermute | solution.py:29
  30.2 0.2 multiply_reduce_fusion
  30.5 4.8 %collective-permute-start.5 = (f32[5,1,128,128]{3,2,1,0:T(8,128)S(1)}, f32[5,1,128,128]{3,2,1,0:T(8,128)S(1)}, u32[]{:S(2)}, u32[]{:S(2)}) collective-permute-start(f32[5,1,128,128]{3,2,1,0:T(8,128)S(1)} %collective-permute-done.4), channel_id=1, source_target_pairs={{0,28},{4,0},{8,4},{12,8},{16,12},{20,16},{24,20},{28,24},{1,29},{... | collective-permute-start | bytes 983048 | tf_op jit(solution)/shard_map/ppermute | solution.py:31
  35.2 7.7 %collective-permute-done.2 = f32[5,1,128,128]{3,2,1,0:T(8,128)S(1)} collective-permute-done((f32[5,1,128,128]{3,2,1,0:T(8,128)S(1)}, f32[5,1,128,128]{3,2,1,0:T(8,128)S(1)}, u32[]{:S(2)}, u32[]{:S(2)}) %collective-permute-start.2) | collective-permute-done | bytes 327712 | tf_op jit(solution)/shard_map/ppermute | solution.py:29
  43.0 2.5 %collective-permute-start.3 = (f32[5,1,128,128]{3,2,1,0:T(8,128)S(1)}, f32[5,1,128,128]{3,2,1,0:T(8,128)S(1)}, u32[]{:S(2)}, u32[]{:S(2)}) collective-permute-start(f32[5,1,128,128]{3,2,1,0:T(8,128)S(1)} %collective-permute-done.2), channel_id=1, source_target_pairs={{0,4},{4,8},{8,12},{12,16},{16,20},{20,24},{24,28},{28,0},{1,5},{5... | collective-permute-start | bytes 983048 | tf_op jit(solution)/shard_map/ppermute | solution.py:29
  45.4 0.7 compare_and_fusion
  46.1 3.1 %collective-permute-start.6 = (f32[5,1,128,128]{3,2,1,0:T(8,128)S(1)}, f32[5,1,128,128]{3,2,1,0:T(8,128)S(1)}, u32[]{:S(2)}, u32[]{:S(2)}) collective-permute-start(f32[5,1,128,128]{3,2,1,0:T(8,128)S(1)} %collective-permute-done.5), channel_id=1, source_target_pairs={{0,28},{4,0},{8,4},{12,8},{16,12},{20,16},{24,20},{28,24},{1,29},{... | collective-permute-start | bytes 983048 | tf_op jit(solution)/shard_map/ppermute | solution.py:31
  49.2 9.7 %collective-permute-done.3 = f32[5,1,128,128]{3,2,1,0:T(8,128)S(1)} collective-permute-done((f32[5,1,128,128]{3,2,1,0:T(8,128)S(1)}, f32[5,1,128,128]{3,2,1,0:T(8,128)S(1)}, u32[]{:S(2)}, u32[]{:S(2)}) %collective-permute-start.3) | collective-permute-done | bytes 327712 | tf_op jit(solution)/shard_map/ppermute | solution.py:29
  59.0 1.0 constant_dynamic-update-slice_fusion.11
  60.1 1.5 %collective-permute-done.6 = f32[5,1,128,128]{3,2,1,0:T(8,128)S(1)} collective-permute-done((f32[5,1,128,128]{3,2,1,0:T(8,128)S(1)}, f32[5,1,128,128]{3,2,1,0:T(8,128)S(1)}, u32[]{:S(2)}, u32[]{:S(2)}) %collective-permute-start.6) | collective-permute-done | bytes 327712 | tf_op jit(solution)/shard_map/ppermute | solution.py:31
  61.9 0.3 constant_dynamic-slice_fusion
  62.2 3.9 %fusion.2 = f32[1,5,128,128]{3,0,2,1:T(1,128)S(1)} fusion(f32[5,8,128,128]{3,2,1,0:T(8,128)S(1)} %constant_dynamic-slice_fusion, f32[8]{0:T(128)S(1)} %get-tuple-element.3), kind=kOutput, calls=%fused_computation.4 | convolution fusion | flops 7864328 | bytes 2949152 | tf_op jit(solution)/shard_map/ij,cjrx->cirx/dot_general | solution.py:134
  66.1 3.9 %fusion = f32[1,5,128,128]{3,0,2,1:T(1,128)S(1)} fusion(f32[5,8,128,128]{3,2,1,0:T(8,128)S(1)} %constant_dynamic-slice_fusion, f32[8]{0:T(128)S(1)} %get-tuple-element.2), kind=kOutput, calls=%fused_computation.2 | convolution fusion | flops 7864336 | bytes 2949152 | tf_op jit(solution)/shard_map/ij,cjrx->cirx/dot_general | solution.py:135
  70.0 0.2 fusion.62
  70.1 1.9 %collective-permute-start.8 = (f32[5,1,128,3]{3,2,1,0:T(8,128)S(1)}, f32[5,1,128,3]{3,2,1,0:T(8,128)S(1)}, u32[]{:S(2)}, u32[]{:S(2)}) collective-permute-start(f32[5,1,128,3]{3,2,1,0:T(8,128)S(1)} %get-tuple-element.7), channel_id=1, source_target_pairs={{0,1},{1,2},{2,3},{4,5},{5,6},{6,7},{8,9},{9,10},{10,11},{12,13},{... | collective-permute-start | bytes 23048 | tf_op jit(solution)/shard_map/ppermute | solution.py:43
  72.1 1.5 %collective-permute-start.7 = (f32[5,1,128,3]{3,2,1,0:T(8,128)S(1)}, f32[5,1,128,3]{3,2,1,0:T(8,128)S(1)}, u32[]{:S(2)}, u32[]{:S(2)}) collective-permute-start(f32[5,1,128,3]{3,2,1,0:T(8,128)S(1)} %get-tuple-element.6), channel_id=1, source_target_pairs={{1,0},{2,1},{3,2},{5,4},{6,5},{7,6},{9,8},{10,9},{11,10},{13,12},{... | collective-permute-start | bytes 23048 | tf_op jit(solution)/shard_map/ppermute | solution.py:44
  73.5 0.1 broadcast_divide_fusion
  73.7 3.0 %collective-permute-done.7 = f32[5,1,128,3]{3,2,1,0:T(8,128)S(1)} collective-permute-done((f32[5,1,128,3]{3,2,1,0:T(8,128)S(1)}, f32[5,1,128,3]{3,2,1,0:T(8,128)S(1)}, u32[]{:S(2)}, u32[]{:S(2)}) %collective-permute-start.7) | collective-permute-done | bytes 7712 | tf_op jit(solution)/shard_map/ppermute | solution.py:44
  76.7 1.1 fusion.9
  78.2 4.7 %copy.13 = f32[5,128,128]{0,2,1:T(8,128)} copy(f32[5,128,128]{2,1,0:T(8,128)S(1)} %multiply_add_fusion) | data formatting | bytes 655360 | tf_op jit(solution)/shard_map/add | solution.py:145
  82.8 4.1 %gather_fusion = f32[256,5]{1,0:T(8,128)S(1)} fusion(f32[5,16384]{0,1:T(8,128)} %bitcast.148, s32[1024]{0:T(1024)S(1)} %pad_clamp_fusion), kind=kCustom, calls=%fused_computation | custom fusion | bytes 11264 | tf_op jit(solution)/shard_map/jit(_take)/gather | solution.py:150
  86.9 0.1 select_bitcast_fusion
  87.1 0.2 fusion.16
  87.3 2.5 %scatter_custom_fusion = f32[256]{0:T(256)S(1)} fusion(s32[256]{0:T(256)} %bitcast.157, f32[256]{0:T(256)S(1)} %compare_select_fusion.4, f32[]{:T(128)} %constant.102.clone.1), kind=kCustom, calls=%fused_computation.119 | custom fusion | flops 256 | bytes 1536 | tf_op jit(solution)/shard_map/scatter-add | solution.py:152
  89.7 42.0 %all-reduce.1 = f32[256]{0:T(256)S(1)} all-reduce(f32[256]{0:T(256)S(1)} %scatter_custom_fusion), channel_id=2, replica_groups=mesh['az'=8,'rx'=4] {'az','rx'}, use_global_device_ids=true, to_apply=%region_3.4.clone | all-reduce | flops 256 | bytes 2048
  131.7 0.6 dynamic-slice
  (41 shorter events, 0.7 us)
Async XLA Ops:
  0.6 61.1 %copy-start.2 = (f32[5,1,128,128]{3,2,1,0:T(8,128)S(1)}, f32[5,1,128,128]{3,2,1,0:T(8,128)}, u32[]{:S(2)}) copy-start(f32[5,1,128,128]{3,2,1,0:T(8,128)} %param.8) | copy-start | bytes 983044
  0.6 17.3 %collective-permute-start = (f32[5,1,128,128]{3,2,1,0:T(8,128)}, f32[5,1,128,128]{3,2,1,0:T(8,128)S(1)}, u32[]{:S(2)}, u32[]{:S(2)}) collective-permute-start(f32[5,1,128,128]{3,2,1,0:T(8,128)} %param.8), channel_id=1, source_target_pairs={{0,4},{4,8},{8,12},{12,16},{16,20},{20,24},{24,28},{28,0},{1,5},{5... | collective-permute-start | bytes 983048 | tf_op jit(solution)/shard_map/ppermute | solution.py:29
  3.6 26.8 %collective-permute-start.4 = (f32[5,1,128,128]{3,2,1,0:T(8,128)}, f32[5,1,128,128]{3,2,1,0:T(8,128)S(1)}, u32[]{:S(2)}, u32[]{:S(2)}) collective-permute-start(f32[5,1,128,128]{3,2,1,0:T(8,128)} %param.8), channel_id=1, source_target_pairs={{0,28},{4,0},{8,4},{12,8},{16,12},{20,16},{24,20},{28,24},{1,29},{... | collective-permute-start | bytes 983048 | tf_op jit(solution)/shard_map/ppermute | solution.py:31
  17.9 12.2 %collective-permute-start.1 = (f32[5,1,128,128]{3,2,1,0:T(8,128)S(1)}, f32[5,1,128,128]{3,2,1,0:T(8,128)S(1)}, u32[]{:S(2)}, u32[]{:S(2)}) collective-permute-start(f32[5,1,128,128]{3,2,1,0:T(8,128)S(1)} %collective-permute-done), channel_id=1, source_target_pairs={{0,4},{4,8},{8,12},{12,16},{16,20},{20,24},{24,28},{28,0},{1,5},{5... | collective-permute-start | bytes 983048 | tf_op jit(solution)/shard_map/ppermute | solution.py:29
  30.2 12.8 %collective-permute-start.2 = (f32[5,1,128,128]{3,2,1,0:T(8,128)S(1)}, f32[5,1,128,128]{3,2,1,0:T(8,128)S(1)}, u32[]{:S(2)}, u32[]{:S(2)}) collective-permute-start(f32[5,1,128,128]{3,2,1,0:T(8,128)S(1)} %collective-permute-done.1), channel_id=1, source_target_pairs={{0,4},{4,8},{8,12},{12,16},{16,20},{20,24},{24,28},{28,0},{1,5},{5... | collective-permute-start | bytes 983048 | tf_op jit(solution)/shard_map/ppermute | solution.py:29
  30.5 15.7 %collective-permute-start.5 = (f32[5,1,128,128]{3,2,1,0:T(8,128)S(1)}, f32[5,1,128,128]{3,2,1,0:T(8,128)S(1)}, u32[]{:S(2)}, u32[]{:S(2)}) collective-permute-start(f32[5,1,128,128]{3,2,1,0:T(8,128)S(1)} %collective-permute-done.4), channel_id=1, source_target_pairs={{0,28},{4,0},{8,4},{12,8},{16,12},{20,16},{24,20},{28,24},{1,29},{... | collective-permute-start | bytes 983048 | tf_op jit(solution)/shard_map/ppermute | solution.py:31
  43.0 16.0 %collective-permute-start.3 = (f32[5,1,128,128]{3,2,1,0:T(8,128)S(1)}, f32[5,1,128,128]{3,2,1,0:T(8,128)S(1)}, u32[]{:S(2)}, u32[]{:S(2)}) collective-permute-start(f32[5,1,128,128]{3,2,1,0:T(8,128)S(1)} %collective-permute-done.2), channel_id=1, source_target_pairs={{0,4},{4,8},{8,12},{12,16},{16,20},{20,24},{24,28},{28,0},{1,5},{5... | collective-permute-start | bytes 983048 | tf_op jit(solution)/shard_map/ppermute | solution.py:29
  46.1 15.5 %collective-permute-start.6 = (f32[5,1,128,128]{3,2,1,0:T(8,128)S(1)}, f32[5,1,128,128]{3,2,1,0:T(8,128)S(1)}, u32[]{:S(2)}, u32[]{:S(2)}) collective-permute-start(f32[5,1,128,128]{3,2,1,0:T(8,128)S(1)} %collective-permute-done.5), channel_id=1, source_target_pairs={{0,28},{4,0},{8,4},{12,8},{16,12},{20,16},{24,20},{28,24},{1,29},{... | collective-permute-start | bytes 983048 | tf_op jit(solution)/shard_map/ppermute | solution.py:31
  62.2 15.6 %copy-start = (f32[3,1,128,128]{3,2,1,0:T(8,128)S(1)}, f32[3,1,128,128]{3,2,1,0:T(8,128)}, u32[]{:S(2)}) copy-start(f32[3,1,128,128]{3,2,1,0:T(8,128)} %param.10) | copy-start | bytes 589828
  62.2 15.7 %copy-start.3 = (f32[1,128,128]{2,1,0:T(8,128)S(1)}, f32[1,128,128]{2,1,0:T(8,128)}, u32[]{:S(2)}) copy-start(f32[1,128,128]{2,1,0:T(8,128)} %param.9) | copy-start | bytes 196612
  62.2 15.7 %copy-start.4 = (f32[1,128,128]{2,1,0:T(8,128)S(1)}, f32[1,128,128]{2,1,0:T(8,128)}, u32[]{:S(2)}) copy-start(f32[1,128,128]{2,1,0:T(8,128)} %param.11) | copy-start | bytes 196612
  70.1 3.5 %collective-permute-start.8 = (f32[5,1,128,3]{3,2,1,0:T(8,128)S(1)}, f32[5,1,128,3]{3,2,1,0:T(8,128)S(1)}, u32[]{:S(2)}, u32[]{:S(2)}) collective-permute-start(f32[5,1,128,3]{3,2,1,0:T(8,128)S(1)} %get-tuple-element.7), channel_id=1, source_target_pairs={{0,1},{1,2},{2,3},{4,5},{5,6},{6,7},{8,9},{9,10},{10,11},{12,13},{... | collective-permute-start | bytes 23048 | tf_op jit(solution)/shard_map/ppermute | solution.py:43
  72.1 4.6 %collective-permute-start.7 = (f32[5,1,128,3]{3,2,1,0:T(8,128)S(1)}, f32[5,1,128,3]{3,2,1,0:T(8,128)S(1)}, u32[]{:S(2)}, u32[]{:S(2)}) collective-permute-start(f32[5,1,128,3]{3,2,1,0:T(8,128)S(1)} %get-tuple-element.6), channel_id=1, source_target_pairs={{1,0},{2,1},{3,2},{5,4},{6,5},{7,6},{9,8},{10,9},{11,10},{13,12},{... | collective-permute-start | bytes 23048 | tf_op jit(solution)/shard_map/ppermute | solution.py:44
  78.1 9.2 %copy-start.5 = (f32[1,1,256]{2,1,0:T(1,128)S(1)}, f32[1,1,256]{2,1,0:T(1,128)}, u32[]{:S(2)}) copy-start(f32[1,1,256]{2,1,0:T(1,128)} %param.14) | copy-start | bytes 3076
  78.1 54.2 %copy-start.1 = (f32[5,128,128]{2,1,0:T(8,128)}, f32[5,128,128]{2,1,0:T(8,128)S(1)}, u32[]{:S(2)}) copy-start(f32[5,128,128]{2,1,0:T(8,128)S(1)} %multiply_add_fusion) | copy-start | bytes 983044
